TPU v7x, 32 devices: a whole 2x2x4 slice. The times are simulated.
32 devices in a mesh: seq: 8 (over y, x, core), ch: 4 (over z).
Axes of the slice: x: 2, y: 2, z: 4, core: 2. Of those that a mesh axis runs over, the one named last changes fastest.
Arguments:
- dna_features: bfloat16 [2, 512, 1280], P(None, 'seq'), may hold values from -6 to 6
- gain_a: float32 [1280], replicated, may hold values from 0.25 to 1.75
- conv_a: bfloat16 [5, 1280, 1408], P(None, 'seq', 'ch'), may hold values from -0.078125 to 0.078125
- bias_a: float32 [1408], P('ch'), may hold values from -3 to 3
- gain_b: float32 [1408], replicated, may hold values from 0.25 to 1.75
- conv_b: bfloat16 [5, 1408, 1536], P(None, 'seq', 'ch'), may hold values from -0.0625 to 0.0625
- bias_b: float32 [1536], P('ch'), may hold values from -3 to 3
- grad_out: bfloat16 [2, 128, 1536], P(None, 'seq', 'ch'), may hold values from -6 to 6
Outputs:
- pooled_out: bfloat16 [2, 128, 1536], P(None, 'seq', 'ch')
- input_grad: bfloat16 [2, 512, 1280], P(None, 'seq', 'ch')
All inputs are finite; a program needn't handle non-finite values.
Results may differ from a plain program's by a relative error of at most 0.018.
Values may be sent and summed in bfloat16 or wider, within the bound.
No kernel may reach another device: no remote copies, remote signals or barrier semaphores. Data moves between devices by JAX's collectives and lax.ppermute only.
A program may use at most 128 MiB of HBM per device.

v0:
```python
import math
import jax
import jax.numpy as jnp
from jax import lax
from jax.sharding import PartitionSpec as P

EPS = 1e-06
ROOT = math.sqrt(2.0 / math.pi)


def with_halo(block, sides, width):
    for axis, dim in sides:
        count = lax.axis_size(axis)
        forward = [(i, i + 1) for i in range(count - 1)]
        backward = [(target, source) for source, target in forward]
        low = lax.ppermute(
            lax.slice_in_dim(block, block.shape[dim] - width, None, axis=dim), axis, forward
        )
        high = lax.ppermute(lax.slice_in_dim(block, 0, width, axis=dim), axis, backward)
        block = jnp.concatenate([low, block, high], axis=dim)
    return block


def gelu_tanh(z):
    return 0.5 * z * (1.0 + jnp.tanh(ROOT * (z + 0.044715 * z * z * z)))


def gelu_slope(z):
    t = jnp.tanh(ROOT * (z + 0.044715 * z * z * z))
    return 0.5 * (1.0 + t) + 0.5 * z * (1.0 - t * t) * ROOT * (1.0 + 3.0 * 0.044715 * z * z)


def pool_pairs(v):
    return v.reshape(v.shape[0], v.shape[1] // 2, 2, v.shape[2]).sum(axis=2) * 0.5


def repeat_half(v):
    return (jnp.repeat(v.astype(jnp.float32), 2, axis=1) * 0.5).astype(jnp.bfloat16)


def conv_rows(padded, weight, length):
    total = jnp.einsum(
        "wtc,co->wto", padded[:, 0:length], weight[0], preferred_element_type=jnp.float32
    )
    for offset in range(1, weight.shape[0]):
        total = total + jnp.einsum(
            "wtc,co->wto",
            padded[:, offset : offset + length],
            weight[offset],
            preferred_element_type=jnp.float32,
        )
    return total


def conv_back(padded, weight, length):
    total = jnp.einsum(
        "wto,co->wtc", padded[:, 4 : 4 + length], weight[0], preferred_element_type=jnp.float32
    )
    for offset in range(1, weight.shape[0]):
        start = 4 - offset
        total = total + jnp.einsum(
            "wto,co->wtc",
            padded[:, start : start + length],
            weight[offset],
            preferred_element_type=jnp.float32,
        )
    return total


def per_device(dna_features, gain_a, conv_a, bias_a, gain_b, conv_b, bias_b, grad_out):
    rows_in = dna_features.shape[1]
    rows_mid = rows_in // 2
    width_in = dna_features.shape[2]
    width_mid = gain_b.shape[0]
    share_mid = bias_a.shape[0]
    share_in = width_in // lax.axis_size("ch")
    ch_index = lax.axis_index("ch")
    whole_a, whole_b = (
        lax.all_gather(conv_a, "seq", axis=1, tiled=True),
        lax.all_gather(conv_b, "seq", axis=1, tiled=True),
    )
    feat = dna_features.astype(jnp.float32)
    scale_a = lax.rsqrt(jnp.mean(feat * feat, axis=-1, keepdims=True) + EPS)
    act_a = gelu_tanh(feat * scale_a * gain_a).astype(jnp.bfloat16)
    padded_a = with_halo(act_a, (("seq", 1),), 2)
    conv_out_a = conv_rows(padded_a, whole_a, rows_in)
    mid = pool_pairs(conv_out_a + bias_a).astype(jnp.bfloat16)
    gain_part = lax.dynamic_slice_in_dim(gain_b, ch_index * share_mid, share_mid, 0)
    mid_f = mid.astype(jnp.float32)
    squares = lax.psum(jnp.sum(mid_f * mid_f, axis=-1, keepdims=True), "ch")
    scale_b = lax.rsqrt(squares / width_mid + EPS)
    act_part = gelu_tanh(mid_f * scale_b * gain_part).astype(jnp.bfloat16)
    act_full = lax.all_gather(act_part, "ch", axis=2, tiled=True)
    padded_b = with_halo(act_full, (("seq", 1),), 2)
    conv_out_b = conv_rows(padded_b, whole_b, rows_mid)
    pooled_out = pool_pairs(conv_out_b + bias_b).astype(jnp.bfloat16)
    grad_b = repeat_half(grad_out)
    grad_pad_b = with_halo(grad_b, (("seq", 1),), 2)
    partial_b = conv_back(grad_pad_b, whole_b, rows_mid)
    back_share = lax.psum_scatter(
        partial_b.astype(jnp.bfloat16), "ch", scatter_dimension=2, tiled=True
    ).astype(jnp.float32)
    normed_b = mid_f * scale_b
    grad_n = back_share * gelu_slope(normed_b * gain_part) * gain_part
    inner_b = lax.psum(jnp.sum(grad_n * normed_b, axis=-1, keepdims=True), "ch") / width_mid
    grad_mid = (scale_b * (grad_n - normed_b * inner_b)).astype(jnp.bfloat16)
    grad_a = repeat_half(grad_mid)
    grad_pad_a = with_halo(grad_a, (("seq", 1),), 2)
    partial_a = conv_back(grad_pad_a, whole_a, rows_in)
    back_share_a = lax.psum_scatter(
        partial_a.astype(jnp.bfloat16), "ch", scatter_dimension=2, tiled=True
    ).astype(jnp.float32)
    feat_part = lax.dynamic_slice_in_dim(feat, ch_index * share_in, share_in, 2)
    gain_part_a = lax.dynamic_slice_in_dim(gain_a, ch_index * share_in, share_in, 0)
    normed_a = feat_part * scale_a
    grad_na = back_share_a * gelu_slope(normed_a * gain_part_a) * gain_part_a
    inner_a = lax.psum(jnp.sum(grad_na * normed_a, axis=-1, keepdims=True), "ch") / width_in
    input_grad = (scale_a * (grad_na - normed_a * inner_a)).astype(jnp.bfloat16)
    return (pooled_out, input_grad)


def solution(mesh):
    in_specs = (
        P(None, "seq", None),
        P(),
        P(None, "seq", "ch"),
        P("ch"),
        P(),
        P(None, "seq", "ch"),
        P("ch"),
        P(None, "seq", "ch"),
    )
    out_specs = (P(None, "seq", "ch"), P(None, "seq", "ch"))
    return jax.shard_map(
        per_device, mesh=mesh, in_specs=in_specs, out_specs=out_specs, check_vma=False
    )
```

profile of v0, /device:TPU:0, one launch (start us, length us, event | category | flops | bytes accessed | tf_op | source)
XLA Modules:
  0.0 215.0 jit_solution(2797888684650728712)
XLA Ops:
  7.2 0.7 all-gather.3.cloned.1.call-update
  7.9 0.7 all-gather.5.cloned.1.call-update
  8.7 1.1 multiply_reduce_fusion
  9.8 1.3 fusion.28
  11.2 1.3 collective-permute-start.1
  12.5 3.0 %collective-permute-start = (bf16[2,2,1280]{2,1,0:T(2,128)(2,1)S(1)}, bf16[2,2,1280]{2,1,0:T(2,128)(2,1)S(1)}, u32[]{:S(2)}, u32[]{:S(2)}) collective-permute-start(bf16[2,2,1280]{2,1,0:T(2,128)(2,1)S(1)} %get-tuple-element.4), channel_id=1, source_target_pairs={{0,4},{4,8},{8,12},{12,16},{16,20},{20,24},{24,28},{1,5},{5,9},{9,... | collective-permute-start | bytes 30728 | tf_op jit(solution)/shard_map/ppermute | solution.py:16
  15.5 0.7 multiply_convert_fusion.3
  16.4 4.5 %collective-permute-start.5 = (bf16[2,2,384]{2,1,0:T(2,128)(2,1)S(1)}, bf16[2,2,384]{2,1,0:T(2,128)(2,1)S(1)}, u32[]{:S(2)}, u32[]{:S(2)}) collective-permute-start(bf16[2,2,384]{2,1,0:T(2,128)(2,1)S(1)} %get-tuple-element.13), channel_id=1, source_target_pairs={{0,4},{4,8},{8,12},{12,16},{16,20},{20,24},{24,28},{1,5},{5,9},{9,... | collective-permute-start | bytes 9224 | tf_op jit(solution)/shard_map/ppermute | solution.py:16
  20.9 1.3 collective-permute-start.4
  22.2 1.0 convert_element_type.60
  23.2 0.8 dynamic_slice.11
  24.0 0.8 dynamic_slice.9
  24.8 27.5 %all-gather.3.cloned.1.call-done = bf16[5,1280,352]{2,1,0:T(8,128)(2,1)} async-done(((bf16[5,160,352]{2,1,0:T(8,128)(2,1)}), bf16[5,1280,352]{2,1,0:T(8,128)(2,1)}) %all-gather.3.cloned.1.call-update) | async-done | bytes 4505616 | tf_op jit(solution)/shard_map/all_gather | solution.py:79
  52.3 1.5 fusion.23
  53.8 1.5 fusion.19
  55.4 1.5 fusion.21
  56.9 1.5 fusion.8
  58.5 1.5 fusion.7
  60.0 0.1 reshape.33
  60.1 0.2 reduce_sum.55
  60.4 35.6 %all-gather.5.cloned.1.call-done = bf16[5,1408,384]{2,1,0:T(8,128)(2,1)} async-done(((bf16[5,176,384]{2,1,0:T(8,128)(2,1)}), bf16[5,1408,384]{2,1,0:T(8,128)(2,1)}) %all-gather.5.cloned.1.call-update) | async-done | bytes 5406736 | tf_op jit(solution)/shard_map/all_gather | solution.py:80
  95.9 1.7 fusion.14
  97.6 1.7 fusion.16
  99.3 1.7 fusion.12
  101.0 1.7 fusion.4
  102.7 1.7 fusion.5
  104.4 1.0 copy.34
  105.5 1.1 reshape.45
  106.6 0.1 fusion.66
  106.7 11.8 %psum.21 = f32[2,32,1]{1,0,2:T(2,128)S(1)} all-reduce(f32[2,32,1]{1,0,2:T(2,128)S(1)} %bitcast.81), channel_id=1, replica_groups=mesh['seq'=8,'ch'=4] {'ch'}, use_global_device_ids=true, to_apply=%region_3.0 | all-reduce | flops 64 | bytes 512 | tf_op jit(solution)/shard_map/psum | solution.py:90
  118.5 8.7 %reduce-scatter.7.cloned.1.call-done = bf16[352,64]{1,0:T(8,128)(2,1)} async-done(((bf16[1408,64]{1,0:T(8,128)(2,1)}), bf16[352,64]{1,0:T(8,128)(2,1)}) %reduce-scatter.7.cloned.1.call-update) | async-done | bytes 45072
  127.3 1.0 reshape.46
  128.3 0.1 copy.35
  128.4 0.2 fusion.62
  128.6 8.8 %psum.22 = f32[2,32,1]{1,0,2:T(2,128)S(1)} all-reduce(f32[2,32,1]{1,0,2:T(2,128)S(1)} %bitcast.82), channel_id=1, replica_groups=mesh['seq'=8,'ch'=4] {'ch'}, use_global_device_ids=true, to_apply=%region_7.0 | all-reduce | flops 64 | bytes 512 | tf_op jit(solution)/shard_map/psum | solution.py:105
  137.5 0.2 multiply_convert_fusion.1
  137.7 0.2 copy.28
  137.8 16.1 %all_gather.10 = bf16[2,32,1408]{1,0,2:T(2,128)(2,1)S(1)} all-gather(bf16[2,32,352]{1,0,2:T(2,128)(2,1)S(1)} %copy.28), channel_id=1, replica_groups=mesh['seq'=8,'ch'=4] {'ch'}, dimensions={2}, use_global_device_ids=true | all-gather | bytes 225280 | tf_op jit(solution)/shard_map/all_gather | solution.py:93
  154.0 0.9 copy.29
  154.9 1.3 collective-permute-start.3
  156.2 3.0 %collective-permute-start.2 = (bf16[2,2,1408]{2,1,0:T(2,128)(2,1)S(1)}, bf16[2,2,1408]{2,1,0:T(2,128)(2,1)S(1)}, u32[]{:S(2)}, u32[]{:S(2)}) collective-permute-start(bf16[2,2,1408]{2,1,0:T(2,128)(2,1)S(1)} %get-tuple-element.6), channel_id=1, source_target_pairs={{0,4},{4,8},{8,12},{12,16},{16,20},{20,24},{24,28},{1,5},{5,9},{9,... | collective-permute-start | bytes 33800 | tf_op jit(solution)/shard_map/ppermute | solution.py:16
  159.3 0.1 convert_element_type.74
  159.4 3.1 %collective-permute-start.7 = (bf16[2,2,352]{2,1,0:T(2,128)(2,1)S(1)}, bf16[2,2,352]{2,1,0:T(2,128)(2,1)S(1)}, u32[]{:S(2)}, u32[]{:S(2)}) collective-permute-start(bf16[2,2,352]{2,1,0:T(2,128)(2,1)S(1)} %get-tuple-element.9), channel_id=1, source_target_pairs={{0,4},{4,8},{8,12},{12,16},{16,20},{20,24},{24,28},{1,5},{5,9},{9,... | collective-permute-start | bytes 8456 | tf_op jit(solution)/shard_map/ppermute | solution.py:16
  162.5 1.3 collective-permute-start.6
  163.8 1.5 fusion.15
  165.4 1.6 fusion.20
  167.0 1.6 fusion.22
  168.7 1.6 fusion.18
  170.3 1.6 fusion.1
  171.9 1.6 fusion.2
  173.6 0.5 copy.36
  174.1 1.0 reshape.47
  175.2 1.5 fusion.13
  176.7 1.5 fusion.11
  178.3 1.5 fusion.17
  179.8 1.5 fusion.10
  181.4 0.1 reduce_sum.57
  181.5 0.6 multiply_convert_fusion.4
  182.1 15.3 %reduce-scatter.9.cloned.1.call-done = bf16[320,128]{1,0:T(8,128)(2,1)} async-done(((bf16[1280,128]{1,0:T(8,128)(2,1)}), bf16[320,128]{1,0:T(8,128)(2,1)}) %reduce-scatter.9.cloned.1.call-update) | async-done | bytes 81936
  197.4 1.0 reshape.48
  198.4 0.1 copy.37
  198.6 0.3 multiply_reduce_fusion.1
  198.9 8.6 %psum.23 = f32[2,64,1]{1,0,2:T(2,128)S(1)} all-reduce(f32[2,64,1]{1,0,2:T(2,128)S(1)} %bitcast.83), channel_id=1, replica_groups=mesh['seq'=8,'ch'=4] {'ch'}, use_global_device_ids=true, to_apply=%region_10.0 | all-reduce | flops 128 | bytes 1024 | tf_op jit(solution)/shard_map/psum | solution.py:117
  207.6 0.9 multiply_convert_fusion
  (34 shorter events, 0.5 us)
Async XLA Ops:
  7.2 45.1 %all-gather.3.cloned.1.call-start = ((), (), s32[]{:S(2)}) async-start(), calls=%async_computation.2 | async-start | bytes 5529600 | tf_op jit(solution)/shard_map/all_gather | solution.py:79
  7.9 88.0 %all-gather.5.cloned.1.call-start = ((), (), s32[]{:S(2)}) async-start(), calls=%async_computation.3 | async-start | bytes 6082560 | tf_op jit(solution)/shard_map/all_gather | solution.py:80
  8.6 118.6 %reduce-scatter.7.cloned.1.call-start = ((), (), s32[]{:S(2)}) async-start(), calls=%async_computation.4 | async-start | bytes 450560
  9.8 48.6 %copy-start = (f32[352]{0:T(512)S(1)}, f32[352]{0:T(512)}, u32[]{:S(2)}) copy-start(f32[352]{0:T(512)} %param.11) | copy-start | bytes 4228
  11.2 13.6 %collective-permute-start.1 = (bf16[2,2,1280]{2,1,0:T(2,128)(2,1)S(1)}, bf16[2,2,1280]{2,1,0:T(2,128)(2,1)S(1)}, u32[]{:S(2)}, u32[]{:S(2)}) collective-permute-start(bf16[2,2,1280]{2,1,0:T(2,128)(2,1)S(1)} %get-tuple-element.5), channel_id=1, source_target_pairs={{4,0},{8,4},{12,8},{16,12},{20,16},{24,20},{28,24},{5,1},{9,5},{13... | collective-permute-start | bytes 30728 | tf_op jit(solution)/shard_map/ppermute | solution.py:19
  12.5 41.3 %collective-permute-start = (bf16[2,2,1280]{2,1,0:T(2,128)(2,1)S(1)}, bf16[2,2,1280]{2,1,0:T(2,128)(2,1)S(1)}, u32[]{:S(2)}, u32[]{:S(2)}) collective-permute-start(bf16[2,2,1280]{2,1,0:T(2,128)(2,1)S(1)} %get-tuple-element.4), channel_id=1, source_target_pairs={{0,4},{4,8},{8,12},{12,16},{16,20},{20,24},{24,28},{1,5},{5,9},{9,... | collective-permute-start | bytes 30728 | tf_op jit(solution)/shard_map/ppermute | solution.py:16
  16.4 81.3 %collective-permute-start.5 = (bf16[2,2,384]{2,1,0:T(2,128)(2,1)S(1)}, bf16[2,2,384]{2,1,0:T(2,128)(2,1)S(1)}, u32[]{:S(2)}, u32[]{:S(2)}) collective-permute-start(bf16[2,2,384]{2,1,0:T(2,128)(2,1)S(1)} %get-tuple-element.13), channel_id=1, source_target_pairs={{0,4},{4,8},{8,12},{12,16},{16,20},{20,24},{24,28},{1,5},{5,9},{9,... | collective-permute-start | bytes 9224 | tf_op jit(solution)/shard_map/ppermute | solution.py:16
  20.9 3.9 %collective-permute-start.4 = (bf16[2,2,384]{2,1,0:T(2,128)(2,1)S(1)}, bf16[2,2,384]{2,1,0:T(2,128)(2,1)S(1)}, u32[]{:S(2)}, u32[]{:S(2)}) collective-permute-start(bf16[2,2,384]{2,1,0:T(2,128)(2,1)S(1)} %get-tuple-element.12), channel_id=1, source_target_pairs={{4,0},{8,4},{12,8},{16,12},{20,16},{24,20},{28,24},{5,1},{9,5},{13... | collective-permute-start | bytes 9224 | tf_op jit(solution)/shard_map/ppermute | solution.py:19
  106.6 90.9 %reduce-scatter.9.cloned.1.call-start = ((), (), s32[]{:S(2)}) async-start(), calls=%async_computation.5 | async-start | bytes 409600
  154.9 23.4 %collective-permute-start.3 = (bf16[2,2,1408]{2,1,0:T(2,128)(2,1)S(1)}, bf16[2,2,1408]{2,1,0:T(2,128)(2,1)S(1)}, u32[]{:S(2)}, u32[]{:S(2)}) collective-permute-start(bf16[2,2,1408]{2,1,0:T(2,128)(2,1)S(1)} %get-tuple-element.7), channel_id=1, source_target_pairs={{4,0},{8,4},{12,8},{16,12},{20,16},{24,20},{28,24},{5,1},{9,5},{13... | collective-permute-start | bytes 33800 | tf_op jit(solution)/shard_map/ppermute | solution.py:19
  156.2 19.0 %collective-permute-start.2 = (bf16[2,2,1408]{2,1,0:T(2,128)(2,1)S(1)}, bf16[2,2,1408]{2,1,0:T(2,128)(2,1)S(1)}, u32[]{:S(2)}, u32[]{:S(2)}) collective-permute-start(bf16[2,2,1408]{2,1,0:T(2,128)(2,1)S(1)} %get-tuple-element.6), channel_id=1, source_target_pairs={{0,4},{4,8},{8,12},{12,16},{16,20},{20,24},{24,28},{1,5},{5,9},{9,... | collective-permute-start | bytes 33800 | tf_op jit(solution)/shard_map/ppermute | solution.py:16
  159.4 7.6 %collective-permute-start.7 = (bf16[2,2,352]{2,1,0:T(2,128)(2,1)S(1)}, bf16[2,2,352]{2,1,0:T(2,128)(2,1)S(1)}, u32[]{:S(2)}, u32[]{:S(2)}) collective-permute-start(bf16[2,2,352]{2,1,0:T(2,128)(2,1)S(1)} %get-tuple-element.9), channel_id=1, source_target_pairs={{0,4},{4,8},{8,12},{12,16},{16,20},{20,24},{24,28},{1,5},{5,9},{9,... | collective-permute-start | bytes 8456 | tf_op jit(solution)/shard_map/ppermute | solution.py:16
  162.5 6.1 %collective-permute-start.6 = (bf16[2,2,352]{2,1,0:T(2,128)(2,1)S(1)}, bf16[2,2,352]{2,1,0:T(2,128)(2,1)S(1)}, u32[]{:S(2)}, u32[]{:S(2)}) collective-permute-start(bf16[2,2,352]{2,1,0:T(2,128)(2,1)S(1)} %get-tuple-element.8), channel_id=1, source_target_pairs={{4,0},{8,4},{12,8},{16,12},{20,16},{24,20},{28,24},{5,1},{9,5},{13... | collective-permute-start | bytes 8456 | tf_op jit(solution)/shard_map/ppermute | solution.py:19
  171.9 7.9 %copy-start.1 = (f32[384]{0:T(512)S(1)}, f32[384]{0:T(512)}, u32[]{:S(2)}) copy-start(f32[384]{0:T(512)} %param.14) | copy-start | bytes 4612
Sparse Core Ops, SparseCore 0:
  9.9 42.3 all-gather.2
  54.2 41.7 all-gather.4
  106.7 20.5 reduce-scatter.6
  175.3 22.1 reduce-scatter.8
where the time goes:
time: 216 us; the launch traced here: 215 us
  waiting for transfers between devices  88.5 us (41%)
  blocking collectives  45.4 us (21%)
  matrix products  31.9 us (15%)
  starting transfers between devices  19 us (9%)
  between operations  14.2 us (7%)
  local copies, waits for them, and re-layouts  8.97 us (4%)
  other arithmetic  6.92 us (3%)
    all_gather x1, waiting for transfers between devices, per_device(): lax.all_gather(conv_b, 'seq', axis=1, tiled=True)  35.6 us
    all_gather x1, waiting for transfers between devices, per_device(): lax.all_gather(conv_a, 'seq', axis=1, tiled=True)  27.5 us
    unnamed x6, waiting for transfers between devices  25.4 us
    all_gather x1, blocking collectives, per_device(): act_full = lax.all_gather(act_part, 'ch', axis=2, tiled=True)  16.1 us
    ppermute x4, starting transfers between devices, with_halo(): lax.ppermute(lax.slice_in_dim(block, block.shape[dim] - width, None, axis...  13.7 us
    dot_general x8, matrix products, conv_back(): jnp.einsum('wto,co->wtc', padded[:, start:start + length], weight[offset]...  13.3 us
    dot_general x8, matrix products, conv_rows(): jnp.einsum('wtc,co->wto', padded[:, offset:offset + length], weight[offse...  12.2 us
    psum x1, blocking collectives, per_device(): squares = lax.psum(jnp.sum(mid_f * mid_f, axis=-1, keepdims=True), 'ch')  11.8 us
  transfers between devices with their start and end apart: 12, of which 4 were waited for; matrix products, arithmetic and copies ran while one was open for 16% of the time, Pallas kernels for 0%

commit v1 on v0

--- a/solution.py
+++ b/solution.py
@@ -6,6 +6,28 @@
 
 EPS = 1e-06
 ROOT = math.sqrt(2.0 / math.pi)
+
+
+def laid_out(blocks, dim):
+    shape = list(blocks.shape[1:])
+    shape[dim] *= blocks.shape[0]
+    return jnp.moveaxis(blocks, 0, dim).reshape(shape)
+
+
+def collect(value, axis, dim):
+    devices = lax.axis_size(axis)
+    pairs = [(i, (i + 1) % devices) for i in range(devices)]
+    back = [(b, a) for a, b in pairs]
+    lower, upper = ([], [])
+    for step in range(devices - 1):
+        if step % 2 == 0:
+            lower.append(lax.ppermute(lower[-1] if lower else value, axis, pairs))
+        else:
+            upper.append(lax.ppermute(upper[-1] if upper else value, axis, back))
+    blocks = jnp.stack([*lower[::-1], value, *upper])
+    shift = lax.axis_index(axis) - len(lower)
+    blocks = blocks[(jnp.arange(devices) - shift) % devices]
+    return laid_out(blocks, dim)
 
 
 def with_halo(block, sides, width):
@@ -77,7 +99,7 @@
     ch_index = lax.axis_index("ch")
     whole_a, whole_b = (
         lax.all_gather(conv_a, "seq", axis=1, tiled=True),
-        lax.all_gather(conv_b, "seq", axis=1, tiled=True),
+        collect(conv_b, "seq", 1),
     )
     feat = dna_features.astype(jnp.float32)
     scale_a = lax.rsqrt(jnp.mean(feat * feat, axis=-1, keepdims=True) + EPS)

time: 216 us -> 263 us (1.22)
  local copies, waits for them, and re-layouts: 8.97 us -> 39.8 us
  waiting for transfers between devices: 88.5 us -> 98.4 us
  matrix products: 31.9 us -> 25.4 us
  other arithmetic: 6.92 us -> 11.9 us
  starting transfers between devices: 19 us -> 23.7 us
    ppermute x0 -> x7, waiting for transfers between devices: none -> 45.1 us  [the longest x4 45.1 us: collect(): lower.append(lax.ppermute(lower[-1] if lower else value, axis, pairs))]
    all_gather x1 -> x0, waiting for transfers between devices: 35.6 us -> none  [per_device(): lax.all_gather(conv_b, 'seq', axis=1, tiled=True)]
    unnamed x14 -> x33, local copies, waits for them, and re-layouts: 5.92 us -> 22 us
    unnamed x6 -> x5, waiting for transfers between devices: 25.4 us -> 33.2 us
    all_gather x1, waiting for transfers between devices: 27.5 us -> 20.1 us  [per_device(): lax.all_gather(conv_a, 'seq', axis=1, tiled=True)]
    ppermute x0 -> x7, starting transfers between devices: none -> 6.82 us  [the longest x3 6.27 us: collect(): upper.append(lax.ppermute(upper[-1] if upper else value, axis, back))]
    gather x0 -> x1, local copies, waits for them, and re-layouts: none -> 6.28 us  [collect(): blocks = blocks[(jnp.arange(devices) - shift) % devices]]
    dot_general x8, matrix products: 13.3 us -> 9.09 us  [conv_back(): jnp.einsum('wto,co->wtc', padded[:, start:start + length], weight[offset]...]
  transfers between devices with their start and end apart: 12 -> 18, of which waited for: 4 -> 7; matrix products, arithmetic and copies ran while one was open for 16% -> 19% of each run, Pallas kernels for 0% -> 0%
where the time goes in v1:
time: 263 us; the launch traced here: 261 us
  waiting for transfers between devices  98.4 us (37%)
  blocking collectives  46.1 us (18%)
  local copies, waits for them, and re-layouts  39.8 us (15%)
  matrix products  25.4 us (10%)
  starting transfers between devices  23.7 us (9%)
  between operations  15.9 us (6%)
  other arithmetic  11.9 us (5%)
    ppermute x4, waiting for transfers between devices, collect(): lower.append(lax.ppermute(lower[-1] if lower else value, axis, pairs))  45.1 us
    unnamed x5, waiting for transfers between devices  33.2 us
    unnamed x33, local copies, waits for them, and re-layouts  22 us
    all_gather x1, waiting for transfers between devices, per_device(): lax.all_gather(conv_a, 'seq', axis=1, tiled=True)  20.1 us
    all_gather x1, blocking collectives, per_device(): act_full = lax.all_gather(act_part, 'ch', axis=2, tiled=True)  17.5 us
    psum x1, blocking collectives, per_device(): squares = lax.psum(jnp.sum(mid_f * mid_f, axis=-1, keepdims=True), 'ch')  11.7 us
    dot_general x8, matrix products, conv_rows(): jnp.einsum('wtc,co->wto', padded[:, offset:offset + length], weight[offse...  11.5 us
    ppermute x4, starting transfers between devices, with_halo(): lax.ppermute(lax.slice_in_dim(block, block.shape[dim] - width, None, axis...  11.4 us
  transfers between devices with their start and end apart: 18, of which 7 were waited for; matrix products, arithmetic and copies ran while one was open for 19% of the time, Pallas kernels for 0%

profile of v1, /device:TPU:0, one launch (start us, length us, event | category | flops | bytes accessed | tf_op | source)
XLA Modules:
  0.0 261.2 jit_solution(12876275843156620395)
XLA Ops:
  8.6 11.6 %collective-permute-done.3 = bf16[5,176,384]{2,1,0:T(8,128)(2,1)S(1)} collective-permute-done((bf16[5,176,384]{2,1,0:T(8,128)(2,1)}, bf16[5,176,384]{2,1,0:T(8,128)(2,1)S(1)}, u32[]{:S(2)}, u32[]{:S(2)}) %collective-permute-start.3) | collective-permute-done | bytes 675872 | tf_op jit(solution)/shard_map/ppermute | solution.py:24
  20.2 2.6 %collective-permute-start.7 = (bf16[5,176,384]{2,1,0:T(8,128)(2,1)}, bf16[5,176,384]{2,1,0:T(8,128)(2,1)S(1)}, u32[]{:S(2)}, u32[]{:S(2)}) collective-permute-start(bf16[5,176,384]{2,1,0:T(8,128)(2,1)} %param.13), channel_id=1, source_target_pairs={{4,0},{8,4},{12,8},{16,12},{20,16},{24,20},{28,24},{0,28},{5,1},{9... | collective-permute-start | bytes 2027528 | tf_op jit(solution)/shard_map/ppermute | solution.py:26
  22.8 13.8 %collective-permute-done.4 = bf16[5,176,384]{2,1,0:T(8,128)(2,1)S(1)} collective-permute-done((bf16[5,176,384]{2,1,0:T(8,128)(2,1)S(1)}, bf16[5,176,384]{2,1,0:T(8,128)(2,1)S(1)}, u32[]{:S(2)}, u32[]{:S(2)}) %collective-permute-start.4) | collective-permute-done | bytes 675872 | tf_op jit(solution)/shard_map/ppermute | solution.py:24
  36.6 2.7 %collective-permute-start.8 = (bf16[5,176,384]{2,1,0:T(8,128)(2,1)S(1)}, bf16[5,176,384]{2,1,0:T(8,128)(2,1)}, u32[]{:S(2)}, u32[]{:S(2)}) collective-permute-start(bf16[5,176,384]{2,1,0:T(8,128)(2,1)S(1)} %collective-permute-done.7), channel_id=1, source_target_pairs={{4,0},{8,4},{12,8},{16,12},{20,16},{24,20},{28,24},{0,28},{5,1},{9... | collective-permute-start | bytes 2027528 | tf_op jit(solution)/shard_map/ppermute | solution.py:26
  39.3 14.5 %collective-permute-done.5 = bf16[5,176,384]{2,1,0:T(8,128)(2,1)} collective-permute-done((bf16[5,176,384]{2,1,0:T(8,128)(2,1)S(1)}, bf16[5,176,384]{2,1,0:T(8,128)(2,1)}, u32[]{:S(2)}, u32[]{:S(2)}) %collective-permute-start.5) | collective-permute-done | bytes 675872 | tf_op jit(solution)/shard_map/ppermute | solution.py:24
  54.6 1.3 collective-permute-start.11
  55.9 3.0 %collective-permute-start.12 = (bf16[2,2,384]{2,1,0:T(2,128)(2,1)S(1)}, bf16[2,2,384]{2,1,0:T(2,128)(2,1)S(1)}, u32[]{:S(2)}, u32[]{:S(2)}) collective-permute-start(bf16[2,2,384]{2,1,0:T(2,128)(2,1)S(1)} %get-tuple-element.18), channel_id=1, source_target_pairs={{0,4},{4,8},{8,12},{12,16},{16,20},{20,24},{24,28},{1,5},{5,9},{9,... | collective-permute-start | bytes 9224 | tf_op jit(solution)/shard_map/ppermute | solution.py:38
  59.1 1.0 collective-permute-start.9
  60.0 5.2 %collective-permute-done.6 = bf16[5,176,384]{2,1,0:T(8,128)(2,1)} collective-permute-done((bf16[5,176,384]{2,1,0:T(8,128)(2,1)}, bf16[5,176,384]{2,1,0:T(8,128)(2,1)}, u32[]{:S(2)}, u32[]{:S(2)}) %collective-permute-start.6) | collective-permute-done | bytes 675872 | tf_op jit(solution)/shard_map/ppermute | solution.py:24
  65.2 2.0 bitcast_dynamic-update-slice_fusion.7
  67.2 2.0 bitcast_dynamic-update-slice_fusion.6
  69.3 0.9 bitcast_dynamic-update-slice_fusion.5
  70.2 0.9 bitcast_dynamic-update-slice_fusion.4
  71.1 0.9 bitcast_dynamic-update-slice_fusion.3
  72.0 0.9 bitcast_dynamic-update-slice_fusion.2
  73.0 2.0 bitcast_dynamic-update-slice_fusion.1
  75.0 0.9 bitcast_dynamic-update-slice_fusion
  75.9 6.3 %gather_fusion = bf16[8,5,176,384]{3,2,1,0:T(8,128)(2,1)} fusion(bf16[8,5,176,384]{3,2,1,0:T(8,128)(2,1)} %bitcast_dynamic-update-slice_fusion, s32[1024]{0:T(1024)S(1)} %pad_clamp_fusion), kind=kCustom, calls=%fused_computation | custom fusion | bytes 10813472 | tf_op jit(solution)/shard_map/gather | solution.py:29
  82.2 3.1 %fusion.90 = (bf16[1,8,176,384]{3,2,0,1:T(8,128)(2,1)S(1)}, bf16[1,8,176,384]{3,2,0,1:T(8,128)(2,1)S(1)}, bf16[1,8,176,384]{3,2,0,1:T(8,128)(2,1)S(1)}, bf16[1,8...) fusion(bf16[5,8,176,384]{3,2,0,1:T(8,128)(2,1)} %bitcast.96), kind=kLoop, calls=%fused_computation.152 | loop fusion | bytes 10813440 | tf_op jit(solution)/shard_map/slice | solution.py:71
  88.2 1.8 copy.34
  90.0 2.7 %reshape.113 = bf16[1408,64]{1,0:T(8,128)(2,1)} reshape(bf16[1408,2,32]{2,1,0:T(2,128)(2,1)} %bitcast.107) | data formatting | bytes 360448
  93.3 1.1 multiply_reduce_fusion
  94.4 1.3 fusion.22
  96.5 2.3 collective-permute-start
  98.8 1.3 collective-permute-start.1
  100.1 1.9 convert_element_type.60
  102.1 0.8 dynamic_slice.9
  102.9 15.7 %reduce-scatter.7.cloned.1.call-done = bf16[352,64]{1,0:T(8,128)(2,1)} async-done(((bf16[1408,64]{1,0:T(8,128)(2,1)}), bf16[352,64]{1,0:T(8,128)(2,1)}) %reduce-scatter.7.cloned.1.call-update) | async-done | bytes 45072
  118.5 1.0 reshape.114
  119.7 20.1 %all-gather.2.cloned.1.call-done = bf16[5,1280,352]{2,1,0:T(8,128)(2,1)} async-done(((bf16[5,160,352]{2,1,0:T(8,128)(2,1)}), bf16[5,1280,352]{2,1,0:T(8,128)(2,1)}) %all-gather.2.cloned.1.call-update) | async-done | bytes 4505616 | tf_op jit(solution)/shard_map/all_gather | solution.py:101
  139.8 1.7 fusion.15
  141.5 1.6 fusion.13
  143.2 1.6 fusion.17
  144.8 1.5 fusion.8
  146.4 2.2 fusion.7
  148.6 1.0 reshape.93
  149.6 0.9 reduce_sum.55
  150.5 1.0 fusion.62
  151.5 11.7 %psum.21 = f32[2,32,1]{1,0,2:T(2,128)S(1)} all-reduce(f32[2,32,1]{1,0,2:T(2,128)S(1)} %bitcast.111), channel_id=1, replica_groups=mesh['seq'=8,'ch'=4] {'ch'}, use_global_device_ids=true, to_apply=%region_3.4 | all-reduce | flops 64 | bytes 512 | tf_op jit(solution)/shard_map/psum | solution.py:112
  163.4 8.4 %psum.22 = f32[2,32,1]{1,0,2:T(2,128)S(1)} all-reduce(f32[2,32,1]{1,0,2:T(2,128)S(1)} %bitcast.112), channel_id=1, replica_groups=mesh['seq'=8,'ch'=4] {'ch'}, use_global_device_ids=true, to_apply=%region_7.8 | all-reduce | flops 64 | bytes 512 | tf_op jit(solution)/shard_map/psum | solution.py:127
  171.8 0.8 multiply_convert_fusion.1
  172.8 17.5 %all_gather.7 = bf16[2,32,1408]{1,0,2:T(2,128)(2,1)} all-gather(bf16[2,32,352]{1,0,2:T(2,128)(2,1)S(1)} %copy.28), channel_id=1, replica_groups=mesh['seq'=8,'ch'=4] {'ch'}, dimensions={2}, use_global_device_ids=true | all-gather | bytes 225280 | tf_op jit(solution)/shard_map/all_gather | solution.py:115
  190.3 2.2 copy.29
  193.1 2.2 fusion.95
  195.3 1.5 broadcast_in_dim.13
  196.7 1.0 convert_element_type.74
  197.7 1.3 collective-permute-start.13
  199.0 3.0 %collective-permute-start.14 = (bf16[2,2,352]{2,1,0:T(2,128)(2,1)S(1)}, bf16[2,2,352]{2,1,0:T(2,128)(2,1)S(1)}, u32[]{:S(2)}, u32[]{:S(2)}) collective-permute-start(bf16[2,2,352]{2,1,0:T(2,128)(2,1)S(1)} %get-tuple-element.14), channel_id=1, source_target_pairs={{0,4},{4,8},{8,12},{12,16},{16,20},{20,24},{24,28},{1,5},{5,9},{9,... | collective-permute-start | bytes 8456 | tf_op jit(solution)/shard_map/ppermute | solution.py:38
  202.1 3.0 %collective-permute-start.2 = (bf16[2,2,1408]{2,1,0:T(2,128)(2,1)}, bf16[2,2,1408]{2,1,0:T(2,128)(2,1)S(1)}, u32[]{:S(2)}, u32[]{:S(2)}) collective-permute-start(bf16[2,2,1408]{2,1,0:T(2,128)(2,1)} %get-tuple-element.11), channel_id=1, source_target_pairs={{0,4},{4,8},{8,12},{12,16},{16,20},{20,24},{24,28},{1,5},{5,9},{9,... | collective-permute-start | bytes 33800 | tf_op jit(solution)/shard_map/ppermute | solution.py:38
  205.1 1.5 collective-permute-start.10
  206.6 1.6 fusion.14
  208.3 1.6 fusion.12
  209.9 1.6 fusion.16
  211.5 1.6 fusion.1
  213.1 2.4 fusion.2
  215.5 2.1 copy.36
  217.6 2.2 reshape.115
  219.8 1.5 fusion.42
  221.3 1.2 fusion.11
  224.0 16.9 %reduce-scatter.9.cloned.1.call-done = bf16[320,128]{1,0:T(8,128)(2,1)} async-done(((bf16[1280,128]{1,0:T(8,128)(2,1)}), bf16[320,128]{1,0:T(8,128)(2,1)}) %reduce-scatter.9.cloned.1.call-update) | async-done | bytes 81936
  240.9 1.0 reshape.116
  242.1 1.3 multiply_reduce_fusion.1
  243.3 8.5 %psum.23 = f32[2,64,1]{1,0,2:T(2,128)S(1)} all-reduce(f32[2,64,1]{1,0,2:T(2,128)S(1)} %bitcast.113), channel_id=1, replica_groups=mesh['seq'=8,'ch'=4] {'ch'}, use_global_device_ids=true, to_apply=%region_10.11 | all-reduce | flops 128 | bytes 1024 | tf_op jit(solution)/shard_map/psum | solution.py:139
  251.9 1.8 multiply_convert_fusion
  (69 shorter events, 8.5 us)
Async XLA Ops:
  8.0 63.1 %copy-start.2 = (bf16[5,176,384]{2,1,0:T(8,128)(2,1)S(1)}, bf16[5,176,384]{2,1,0:T(8,128)(2,1)}, u32[]{:S(2)}) copy-start(bf16[5,176,384]{2,1,0:T(8,128)(2,1)} %param.13) | copy-start | bytes 2027524
  8.0 110.5 %reduce-scatter.7.cloned.1.call-start = ((), (), s32[]{:S(2)}) async-start(), calls=%async_computation.3 | async-start | bytes 450560
  8.1 12.1 %collective-permute-start.3 = (bf16[5,176,384]{2,1,0:T(8,128)(2,1)}, bf16[5,176,384]{2,1,0:T(8,128)(2,1)S(1)}, u32[]{:S(2)}, u32[]{:S(2)}) collective-permute-start(bf16[5,176,384]{2,1,0:T(8,128)(2,1)} %param.13), channel_id=1, source_target_pairs={{0,4},{4,8},{8,12},{12,16},{16,20},{20,24},{24,28},{28,0},{1,5},{5... | collective-permute-start | bytes 2027528 | tf_op jit(solution)/shard_map/ppermute | solution.py:24
  20.2 16.5 %collective-permute-start.4 = (bf16[5,176,384]{2,1,0:T(8,128)(2,1)S(1)}, bf16[5,176,384]{2,1,0:T(8,128)(2,1)S(1)}, u32[]{:S(2)}, u32[]{:S(2)}) collective-permute-start(bf16[5,176,384]{2,1,0:T(8,128)(2,1)S(1)} %collective-permute-done.3), channel_id=1, source_target_pairs={{0,4},{4,8},{8,12},{12,16},{16,20},{20,24},{24,28},{28,0},{1,5},{5... | collective-permute-start | bytes 2027528 | tf_op jit(solution)/shard_map/ppermute | solution.py:24
  20.2 16.5 %collective-permute-start.7 = (bf16[5,176,384]{2,1,0:T(8,128)(2,1)}, bf16[5,176,384]{2,1,0:T(8,128)(2,1)S(1)}, u32[]{:S(2)}, u32[]{:S(2)}) collective-permute-start(bf16[5,176,384]{2,1,0:T(8,128)(2,1)} %param.13), channel_id=1, source_target_pairs={{4,0},{8,4},{12,8},{16,12},{20,16},{24,20},{28,24},{0,28},{5,1},{9... | collective-permute-start | bytes 2027528 | tf_op jit(solution)/shard_map/ppermute | solution.py:26
  36.6 17.2 %collective-permute-start.5 = (bf16[5,176,384]{2,1,0:T(8,128)(2,1)S(1)}, bf16[5,176,384]{2,1,0:T(8,128)(2,1)}, u32[]{:S(2)}, u32[]{:S(2)}) collective-permute-start(bf16[5,176,384]{2,1,0:T(8,128)(2,1)S(1)} %collective-permute-done.4), channel_id=1, source_target_pairs={{0,4},{4,8},{8,12},{12,16},{16,20},{20,24},{24,28},{28,0},{1,5},{5... | collective-permute-start | bytes 2027528 | tf_op jit(solution)/shard_map/ppermute | solution.py:24
  36.6 22.4 %collective-permute-start.8 = (bf16[5,176,384]{2,1,0:T(8,128)(2,1)S(1)}, bf16[5,176,384]{2,1,0:T(8,128)(2,1)}, u32[]{:S(2)}, u32[]{:S(2)}) collective-permute-start(bf16[5,176,384]{2,1,0:T(8,128)(2,1)S(1)} %collective-permute-done.7), channel_id=1, source_target_pairs={{4,0},{8,4},{12,8},{16,12},{20,16},{24,20},{28,24},{0,28},{5,1},{9... | collective-permute-start | bytes 2027528 | tf_op jit(solution)/shard_map/ppermute | solution.py:26
  53.8 11.4 %collective-permute-start.6 = (bf16[5,176,384]{2,1,0:T(8,128)(2,1)}, bf16[5,176,384]{2,1,0:T(8,128)(2,1)}, u32[]{:S(2)}, u32[]{:S(2)}) collective-permute-start(bf16[5,176,384]{2,1,0:T(8,128)(2,1)} %collective-permute-done.5), channel_id=1, source_target_pairs={{0,4},{4,8},{8,12},{12,16},{16,20},{20,24},{24,28},{28,0},{1,5},{5... | collective-permute-start | bytes 2027528 | tf_op jit(solution)/shard_map/ppermute | solution.py:24
  54.6 4.4 %collective-permute-start.11 = (bf16[2,2,384]{2,1,0:T(2,128)(2,1)S(1)}, bf16[2,2,384]{2,1,0:T(2,128)(2,1)S(1)}, u32[]{:S(2)}, u32[]{:S(2)}) collective-permute-start(bf16[2,2,384]{2,1,0:T(2,128)(2,1)S(1)} %get-tuple-element.17), channel_id=1, source_target_pairs={{4,0},{8,4},{12,8},{16,12},{20,16},{24,20},{28,24},{5,1},{9,5},{13... | collective-permute-start | bytes 9224 | tf_op jit(solution)/shard_map/ppermute | solution.py:41
  55.9 31.3 %collective-permute-start.12 = (bf16[2,2,384]{2,1,0:T(2,128)(2,1)S(1)}, bf16[2,2,384]{2,1,0:T(2,128)(2,1)S(1)}, u32[]{:S(2)}, u32[]{:S(2)}) collective-permute-start(bf16[2,2,384]{2,1,0:T(2,128)(2,1)S(1)} %get-tuple-element.18), channel_id=1, source_target_pairs={{0,4},{4,8},{8,12},{12,16},{16,20},{20,24},{24,28},{1,5},{5,9},{9,... | collective-permute-start | bytes 9224 | tf_op jit(solution)/shard_map/ppermute | solution.py:38
  59.1 15.9 %collective-permute-start.9 = (bf16[5,176,384]{2,1,0:T(8,128)(2,1)}, bf16[5,176,384]{2,1,0:T(8,128)(2,1)S(1)}, u32[]{:S(2)}, u32[]{:S(2)}) collective-permute-start(bf16[5,176,384]{2,1,0:T(8,128)(2,1)} %collective-permute-done.8), channel_id=1, source_target_pairs={{4,0},{8,4},{12,8},{16,12},{20,16},{24,20},{28,24},{0,28},{5,1},{9... | collective-permute-start | bytes 2027528 | tf_op jit(solution)/shard_map/ppermute | solution.py:26
  85.3 1.0 copy-start
  85.3 1.5 copy-start.1
  86.3 8.1 %copy-start.5 = (f32[1280]{0:T(1024)S(1)}, f32[1280]{0:T(1024)}, u32[]{:S(2)}) copy-start(f32[1280]{0:T(1024)} %param.9) | copy-start | bytes 15364
  92.7 47.1 %all-gather.2.cloned.1.call-start = ((), (), s32[]{:S(2)}) async-start(), calls=%async_computation.2 | async-start | bytes 5529600 | tf_op jit(solution)/shard_map/all_gather | solution.py:101
  93.3 147.7 %reduce-scatter.9.cloned.1.call-start = ((), (), s32[]{:S(2)}) async-start(), calls=%async_computation.4 | async-start | bytes 409600
  94.4 51.9 %copy-start.7 = (f32[352]{0:T(512)S(1)}, f32[352]{0:T(512)}, u32[]{:S(2)}) copy-start(f32[352]{0:T(512)} %param.11) | copy-start | bytes 4228
  95.8 0.7 copy-start.3
  96.5 45.0 %collective-permute-start = (bf16[2,2,1280]{2,1,0:T(2,128)(2,1)S(1)}, bf16[2,2,1280]{2,1,0:T(2,128)(2,1)S(1)}, u32[]{:S(2)}, u32[]{:S(2)}) collective-permute-start(bf16[2,2,1280]{2,1,0:T(2,128)(2,1)S(1)} %get-tuple-element.9), channel_id=1, source_target_pairs={{0,4},{4,8},{8,12},{12,16},{16,20},{20,24},{24,28},{1,5},{5,9},{9,... | collective-permute-start | bytes 30728 | tf_op jit(solution)/shard_map/ppermute | solution.py:38
  98.8 44.4 %collective-permute-start.1 = (bf16[2,2,1280]{2,1,0:T(2,128)(2,1)S(1)}, bf16[2,2,1280]{2,1,0:T(2,128)(2,1)S(1)}, u32[]{:S(2)}, u32[]{:S(2)}) collective-permute-start(bf16[2,2,1280]{2,1,0:T(2,128)(2,1)S(1)} %get-tuple-element.10), channel_id=1, source_target_pairs={{4,0},{8,4},{12,8},{16,12},{20,16},{24,20},{28,24},{5,1},{9,5},{13... | collective-permute-start | bytes 30728 | tf_op jit(solution)/shard_map/ppermute | solution.py:41
  139.8 5.0 %copy-start.4 = (bf16[2,64,1280]{2,1,0:T(8,128)(2,1)S(1)}, bf16[2,64,1280]{2,1,0:T(8,128)(2,1)}, u32[]{:S(2)}) copy-start(bf16[2,64,1280]{2,1,0:T(8,128)(2,1)} %copy-done.3) | copy-start | bytes 983044
  197.7 10.5 %collective-permute-start.13 = (bf16[2,2,352]{2,1,0:T(2,128)(2,1)S(1)}, bf16[2,2,352]{2,1,0:T(2,128)(2,1)S(1)}, u32[]{:S(2)}, u32[]{:S(2)}) collective-permute-start(bf16[2,2,352]{2,1,0:T(2,128)(2,1)S(1)} %get-tuple-element.13), channel_id=1, source_target_pairs={{4,0},{8,4},{12,8},{16,12},{20,16},{24,20},{28,24},{5,1},{9,5},{13... | collective-permute-start | bytes 8456 | tf_op jit(solution)/shard_map/ppermute | solution.py:41
  199.0 10.8 %collective-permute-start.14 = (bf16[2,2,352]{2,1,0:T(2,128)(2,1)S(1)}, bf16[2,2,352]{2,1,0:T(2,128)(2,1)S(1)}, u32[]{:S(2)}, u32[]{:S(2)}) collective-permute-start(bf16[2,2,352]{2,1,0:T(2,128)(2,1)S(1)} %get-tuple-element.14), channel_id=1, source_target_pairs={{0,4},{4,8},{8,12},{12,16},{16,20},{20,24},{24,28},{1,5},{5,9},{9,... | collective-permute-start | bytes 8456 | tf_op jit(solution)/shard_map/ppermute | solution.py:38
  202.1 17.7 %collective-permute-start.2 = (bf16[2,2,1408]{2,1,0:T(2,128)(2,1)}, bf16[2,2,1408]{2,1,0:T(2,128)(2,1)S(1)}, u32[]{:S(2)}, u32[]{:S(2)}) collective-permute-start(bf16[2,2,1408]{2,1,0:T(2,128)(2,1)} %get-tuple-element.11), channel_id=1, source_target_pairs={{0,4},{4,8},{8,12},{12,16},{16,20},{20,24},{24,28},{1,5},{5,9},{9,... | collective-permute-start | bytes 33800 | tf_op jit(solution)/shard_map/ppermute | solution.py:38
  205.1 17.4 %collective-permute-start.10 = (bf16[2,2,1408]{2,1,0:T(2,128)(2,1)}, bf16[2,2,1408]{2,1,0:T(2,128)(2,1)S(1)}, u32[]{:S(2)}, u32[]{:S(2)}) collective-permute-start(bf16[2,2,1408]{2,1,0:T(2,128)(2,1)} %get-tuple-element.12), channel_id=1, source_target_pairs={{4,0},{8,4},{12,8},{16,12},{20,16},{24,20},{28,24},{5,1},{9,5},{13... | collective-permute-start | bytes 33800 | tf_op jit(solution)/shard_map/ppermute | solution.py:41
  215.5 7.3 %copy-start.6 = (f32[384]{0:T(512)S(1)}, f32[384]{0:T(512)}, u32[]{:S(2)}) copy-start(f32[384]{0:T(512)} %param.14) | copy-start | bytes 4612
Sparse Core Ops, SparseCore 0:
  92.8 25.6 reduce-scatter.6
  219.9 20.9 reduce-scatter.8
Sparse Core Ops, SparseCore 1:
  95.1 44.7 all-gather.1
